TPU v7x, 128 devices: a whole 4x4x4 slice. The times are simulated.
128 devices in a mesh: grp: 4 (over z), ctx: 32 (over x, y, core).
Axes of the slice: x: 4, y: 4, z: 4, core: 2. Of those that a mesh axis runs over, the one named last changes fastest.
Arguments:
- queries: bfloat16 [49152, 1024], P(('grp', 'ctx')), may hold values from -10 to 10
- keys_cache: bfloat16 [16384, 128, 128], P(('grp', 'ctx')), may hold values from -8 to 8
- values_cache: bfloat16 [16384, 128, 128], P(('grp', 'ctx')), may hold values from -6 to 6
- block_list: int32 [384, 36], P(('grp', 'ctx')), may hold values from 0 to 16383, as said below
- page_table: int32 [16384], replicated, may hold values from 0 to 16383, as said below
Outputs:
- attended: bfloat16 [49152, 1024], P(('grp', 'ctx'))
Inputs may be any that keep to these rules, and one draw needn't show every extreme that they name: `block_list`: each tile's 36 listed blocks are distinct. Page p is row p of keys_cache and values_cache. Through page_table, each tile lists exactly 9 blocks stored on the devices of each index of grp. Over the 3 tiles of one device and one index of grp, at most 3 listed blocks are stored on any one device, and in every draw, for every device and every group, some device of that group stores exactly 3 of them. `page_table`: each page once.
All inputs are finite; a program needn't handle non-finite values.
Results may differ from a plain program's by a relative error of at most 0.0045.
Values may be sent and summed in bfloat16 or wider, within the bound.
A program may use at most 192 MiB of HBM per device.

v0:
```python
import jax
import jax.numpy as jnp
from jax import lax
from jax.sharding import PartitionSpec as P

HD = 128
HEADS = 8
BLOCK = 128
NB = 36
TILE_DEV = 3
BLK_DEV = 128


def owner_plan(page_ids, device_count, capacity):
    tile_count = page_ids.shape[0]
    flattened = page_ids.reshape(-1)
    device_of = flattened // BLK_DEV
    within = flattened % BLK_DEV
    position = jnp.arange(flattened.shape[0], dtype=jnp.int32)
    earlier = (device_of[None, :] == device_of[:, None]) & (position[None, :] < position[:, None])
    rank_index = jnp.sum(earlier.astype(jnp.int32), axis=1)
    slot_index = device_of * capacity + rank_index
    wanted_pages = (
        jnp.zeros((device_count * capacity,), jnp.int32).at[slot_index].set(within, mode="drop")
    )
    return (wanted_pages, slot_index.reshape(tile_count, NB))


def lookup(requested, keys_cache, values_cache):
    return jnp.stack((keys_cache[requested], values_cache[requested]), axis=2)


def empty_state(tile_count, rows_count):
    return (
        jnp.zeros((tile_count, rows_count, HD), jnp.float32),
        jnp.full((tile_count, rows_count), -jnp.inf, jnp.float32),
        jnp.zeros((tile_count, rows_count), jnp.float32),
    )


def block_scores(query_rows, chosen, scaling):
    tile_count = chosen.shape[0]
    keys_now = chosen[:, :, 0].reshape(tile_count, -1, HD)
    return (
        jnp.einsum("tqd,tkd->tqk", query_rows, keys_now, preferred_element_type=jnp.float32)
        * scaling
    )


def attend_block(query_rows, chosen, carried, scaling):
    weighted, running_max, denominator = carried
    tile_count = chosen.shape[0]
    values_now = chosen[:, :, 1].reshape(tile_count, -1, HD)
    scores = block_scores(query_rows, chosen, scaling)
    new_max = jnp.max(scores, axis=2)
    weights = jnp.exp(scores - new_max[:, :, None])
    fading = jnp.exp(running_max - new_max)
    denominator = denominator * fading + jnp.sum(weights, axis=2)
    weighted = weighted * fading[:, :, None] + jnp.einsum(
        "tqk,tkd->tqd", weights.astype(jnp.bfloat16), values_now, preferred_element_type=jnp.float32
    )
    return (weighted, new_max, denominator)


def on_device(queries, keys_cache, values_cache, block_list, page_table):
    groups = lax.axis_size("grp")
    ctx_count = lax.axis_size("ctx")
    per_grp = NB // groups
    capacity = max(3, (2 * TILE_DEV * per_grp + ctx_count - 1) // ctx_count)
    scaling = HD ** (-0.5)
    rows_count = HEADS * BLOCK
    query_rows = (
        queries.reshape(TILE_DEV, BLOCK, HEADS, HD)
        .transpose(0, 2, 1, 3)
        .reshape(TILE_DEV, rows_count, HD)
    )
    device_count = groups * ctx_count
    own_pages = page_table[block_list]
    wanted_pages, picked = owner_plan(own_pages, device_count, capacity)
    requested = lax.all_to_all(
        wanted_pages.reshape(device_count, capacity),
        ("grp", "ctx"),
        split_axis=0,
        concat_axis=0,
        tiled=True,
    )
    fetched = lax.all_to_all(
        lookup(requested, keys_cache, values_cache),
        ("grp", "ctx"),
        split_axis=0,
        concat_axis=0,
        tiled=True,
    )
    fetched = fetched.reshape(device_count * capacity, 2, BLOCK, HD)

    def single(operands):
        rows_one, picked_one = operands
        state = attend_block(
            rows_one[None], fetched[picked_one][None], empty_state(1, rows_count), scaling
        )
        return (state[0][0], state[1][0], state[2][0])

    weighted, running_max, denominator = lax.map(single, (query_rows, picked))
    attended = (
        (weighted / denominator[:, :, None])
        .reshape(TILE_DEV, HEADS, BLOCK, HD)
        .transpose(0, 2, 1, 3)
        .reshape(TILE_DEV * BLOCK, HEADS * HD)
    )
    return attended.astype(jnp.bfloat16)


def solution(mesh):
    in_specs = (
        P(("grp", "ctx"), None),
        P(("grp", "ctx"), None, None),
        P(("grp", "ctx"), None, None),
        P(("grp", "ctx"), None),
        P(),
    )
    out_specs = P(("grp", "ctx"), None)
    return jax.shard_map(
        on_device, mesh=mesh, in_specs=in_specs, out_specs=out_specs, check_vma=False
    )
```

profile of v0, /device:TPU:50, one launch (start us, length us, event | category | flops | bytes accessed | tf_op | source)
XLA Modules:
  0.0 544.1 jit_solution(17062618644644428543)
XLA Ops:
  0.0 0.0 copy-start
  0.0 0.7 compare_select_fusion.2
  0.7 0.1 reshape.288
  0.8 0.0 copy-done
  0.8 1.1 gather_fusion.1
  2.0 0.2 convert_reduce_fusion
  2.2 0.9 scatter_custom_fusion
  3.1 0.2 all_to_all.11
  3.3 15.8 %all_to_all.17 = s32[128,1,3]{2,1,0:T(1,128)S(1)} all-to-all(s32[128,1,3]{2,1,0:T(1,128)S(1)} %bitcast.94), channel_id=1, replica_groups=mesh['grp'=4,'ctx'=32] {'grp','ctx'}, dimensions={0} | all-to-all | bytes 3072 | tf_op jit(solution)/shard_map/all_to_all | solution.py:80
  19.2 0.2 reshape.296
  19.4 13.0 %gather_fusion.2 = bf16[384,128,128]{2,1,0:T(8,128)(2,1)} fusion(bf16[128,128,128]{2,1,0:T(8,128)(2,1)} %param.8, s32[1024]{0:T(1024)S(1)} %pad_clamp_fusion.1), kind=kCustom, calls=%fused_computation.2 | custom fusion | bytes 25167360 | tf_op jit(solution)/shard_map/gather | solution.py:30
  32.4 13.1 %gather_fusion.3 = bf16[384,128,128]{2,1,0:T(8,128)(2,1)} fusion(bf16[128,128,128]{2,1,0:T(8,128)(2,1)} %param.9, s32[1024]{0:T(1024)S(1)} %pad_clamp_fusion.1), kind=kCustom, calls=%fused_computation.3 | custom fusion | bytes 25167360 | tf_op jit(solution)/shard_map/gather | solution.py:30
  45.4 20.7 %pad_maximum_fusion = bf16[128,3,2,128,128]{4,3,2,1,0:T(8,128)(2,1)} fusion(bf16[128,3,1,128,128]{4,3,2,1,0:T(8,128)(2,1)} %bitcast.86, bf16[128,3,1,128,128]{4,3,2,1,0:T(8,128)(2,1)} %bitcast.85), kind=kLoop, calls=%fused_computation.25 | loop fusion | flops 12582912 | bytes 50331648 | tf_op jit(solution)/shard_map/stack | solution.py:30
  66.1 0.0 copy-start.3
  66.1 9.6 %all-to-all-start.1 = ((bf16[128,3,2,128,128]{4,3,2,1,0:T(8,128)(2,1)}), bf16[128,3,2,128,128]{4,3,2,1,0:T(8,128)(2,1)}, u32[]{:S(2)}, u32[]{:S(2)}) async-start(bf16[128,3,2,128,128]{4,3,2,1,0:T(8,128)(2,1)} %pad_maximum_fusion), calls=%async_computation.1 | async-start | bytes 50331648 | tf_op jit(solution)/shard_map/all_to_all | solution.py:87
  75.6 0.1 reduce_sum.23
  75.7 0.1 reshape.287
  75.8 0.0 copy-done.3
  75.8 0.2 copy.24
  76.0 0.2 copy.19
  76.2 349.1 %all-to-all-done.1 = bf16[128,3,2,128,128]{4,3,2,1,0:T(8,128)(2,1)} async-done(((bf16[128,3,2,128,128]{4,3,2,1,0:T(8,128)(2,1)}), bf16[128,3,2,128,128]{4,3,2,1,0:T(8,128)(2,1)}, u32[]{:S(2)}, u32[]{:S(2)}) %all-to-all-start.1) | async-done | bytes 25165856 | tf_op jit(solution)/shard_map/all_to_all | solution.py:87
  425.3 115.3 %while.12 = (s32[]{:T(128)}, f32[3,1024,128]{2,1,0:T(8,128)}, f32[3,1024]{1,0:T(4,128)S(1)}, bf16[3,1024,128]{2,1,0:T(8,128)(2,1)S(1)}, s32[3,36]{1,0:T(4,128)S(...) while((s32[]{:T(128)}, f32[3,1024,128]{2,1,0:T(8,128)}, f32[3,1024]{1,0:T(4,128)S(1)}, ...), condition=%wide.region_5.6_spmd, body=%wide.region_2.5_spmd.sunk | while | flops 2453800960 | bytes 73974968 | solution.py:103
  425.3 9.2 %gather_fusion = bf16[36,2,128,128]{3,2,1,0:T(8,128)(2,1)S(1)} fusion(bf16[384,2,128,128]{3,2,1,0:T(8,128)(2,1)} %get-tuple-element.130, s32[1024]{0:T(1024)S(1)} %pad_clamp_fusion.4), kind=kCustom, calls=%fused_computation.clone.1 | custom fusion | bytes 4718736 | tf_op jit(solution)/shard_map/while/body/eval_jaxpr/gather | solution.py:99
  434.5 1.2 fusion.44
  435.6 7.9 %multiply_reduce_fusion.2 = (f32[1024]{0:T(1024)S(1)}, f32[1024,4608]{1,0:T(8,128)}) fusion(bf16[4608,128]{1,0:T(8,128)(2,1)S(1)} %bitcast.84, bf16[3,1024,128]{2,1,0:T(8,128)(2,1)S(1)} %get-tuple-element.128, s32[]{:T(128)} %get-tuple-element.117), kind=kOutput, calls=%fused_computation.6.clone.1 | convolution fusion | flops 1217395712 | bytes 20320260 | tf_op jit(solution)/shard_map/while/body/eval_jaxpr/tqd,tkd->tqk/dot_general | solution.py:45
  443.5 0.0 copy-start.2
  443.5 9.6 %fusion.45 = f32[1024]{0:T(1024)S(1)} fusion(f32[1024,4608]{1,0:T(8,128)} %get-tuple-element.105, f32[1024]{0:T(1024)S(1)} %get-tuple-element.106), kind=kLoop, calls=%fused_computation.7.clone.1 | loop fusion | flops 14154752 | bytes 18882560 | tf_op jit(solution)/shard_map/while/body/eval_jaxpr/reduce_sum | solution.py:58
  453.2 0.0 copy-done.2
  453.2 10.5 %fusion.47 = f32[3,1024,128]{2,1,0:T(8,128)} fusion(f32[3,1024,128]{2,1,0:T(8,128)} %get-tuple-element.118, s32[]{:T(128)} %get-tuple-element.117, bf16[4608,128]{1,0:T(8,128)(2,1)S(1)} %bitcast.87, f32[1024,4608]{1,0:T(8,128)} %get-tuple-element.105, f32[1024]{0:T(1024)S(1)} %get-tuple-element.106, f32[1024]{0:T(1024)S(1)} %get-tuple-element.107), kind=kOutput, calls=%fused_computation.12.clone.1 | convolution fusion | flops 1222246400 | bytes 20587008 | tf_op jit(solution)/shard_map/while/body/eval_jaxpr/tqk,tkd->tqd/dot_general | solution.py:59
  463.7 9.2 %gather_fusion = bf16[36,2,128,128]{3,2,1,0:T(8,128)(2,1)S(1)} fusion(bf16[384,2,128,128]{3,2,1,0:T(8,128)(2,1)} %get-tuple-element.130, s32[1024]{0:T(1024)S(1)} %pad_clamp_fusion.4), kind=kCustom, calls=%fused_computation.clone.1 | custom fusion | bytes 4718736 | tf_op jit(solution)/shard_map/while/body/eval_jaxpr/gather | solution.py:99
  472.9 1.2 fusion.44
  474.1 7.9 %multiply_reduce_fusion.2 = (f32[1024]{0:T(1024)S(1)}, f32[1024,4608]{1,0:T(8,128)}) fusion(bf16[4608,128]{1,0:T(8,128)(2,1)S(1)} %bitcast.84, bf16[3,1024,128]{2,1,0:T(8,128)(2,1)S(1)} %get-tuple-element.128, s32[]{:T(128)} %get-tuple-element.117), kind=kOutput, calls=%fused_computation.6.clone.1 | convolution fusion | flops 1217395712 | bytes 20320260 | tf_op jit(solution)/shard_map/while/body/eval_jaxpr/tqd,tkd->tqk/dot_general | solution.py:45
  482.0 0.0 copy-start.2
  482.0 9.6 %fusion.45 = f32[1024]{0:T(1024)S(1)} fusion(f32[1024,4608]{1,0:T(8,128)} %get-tuple-element.105, f32[1024]{0:T(1024)S(1)} %get-tuple-element.106), kind=kLoop, calls=%fused_computation.7.clone.1 | loop fusion | flops 14154752 | bytes 18882560 | tf_op jit(solution)/shard_map/while/body/eval_jaxpr/reduce_sum | solution.py:58
  491.6 0.0 copy-done.2
  491.6 10.5 %fusion.47 = f32[3,1024,128]{2,1,0:T(8,128)} fusion(f32[3,1024,128]{2,1,0:T(8,128)} %get-tuple-element.118, s32[]{:T(128)} %get-tuple-element.117, bf16[4608,128]{1,0:T(8,128)(2,1)S(1)} %bitcast.87, f32[1024,4608]{1,0:T(8,128)} %get-tuple-element.105, f32[1024]{0:T(1024)S(1)} %get-tuple-element.106, f32[1024]{0:T(1024)S(1)} %get-tuple-element.107), kind=kOutput, calls=%fused_computation.12.clone.1 | convolution fusion | flops 1222246400 | bytes 20587008 | tf_op jit(solution)/shard_map/while/body/eval_jaxpr/tqk,tkd->tqd/dot_general | solution.py:59
  502.2 9.2 %gather_fusion = bf16[36,2,128,128]{3,2,1,0:T(8,128)(2,1)S(1)} fusion(bf16[384,2,128,128]{3,2,1,0:T(8,128)(2,1)} %get-tuple-element.130, s32[1024]{0:T(1024)S(1)} %pad_clamp_fusion.4), kind=kCustom, calls=%fused_computation.clone.1 | custom fusion | bytes 4718736 | tf_op jit(solution)/shard_map/while/body/eval_jaxpr/gather | solution.py:99
  511.4 1.2 fusion.44
  512.5 7.9 %multiply_reduce_fusion.2 = (f32[1024]{0:T(1024)S(1)}, f32[1024,4608]{1,0:T(8,128)}) fusion(bf16[4608,128]{1,0:T(8,128)(2,1)S(1)} %bitcast.84, bf16[3,1024,128]{2,1,0:T(8,128)(2,1)S(1)} %get-tuple-element.128, s32[]{:T(128)} %get-tuple-element.117), kind=kOutput, calls=%fused_computation.6.clone.1 | convolution fusion | flops 1217395712 | bytes 20320260 | tf_op jit(solution)/shard_map/while/body/eval_jaxpr/tqd,tkd->tqk/dot_general | solution.py:45
  520.4 0.0 copy-start.2
  520.4 9.6 %fusion.45 = f32[1024]{0:T(1024)S(1)} fusion(f32[1024,4608]{1,0:T(8,128)} %get-tuple-element.105, f32[1024]{0:T(1024)S(1)} %get-tuple-element.106), kind=kLoop, calls=%fused_computation.7.clone.1 | loop fusion | flops 14154752 | bytes 18882560 | tf_op jit(solution)/shard_map/while/body/eval_jaxpr/reduce_sum | solution.py:58
  530.1 0.0 copy-done.2
  530.1 10.4 %fusion.47 = f32[3,1024,128]{2,1,0:T(8,128)} fusion(f32[3,1024,128]{2,1,0:T(8,128)} %get-tuple-element.118, s32[]{:T(128)} %get-tuple-element.117, bf16[4608,128]{1,0:T(8,128)(2,1)S(1)} %bitcast.87, f32[1024,4608]{1,0:T(8,128)} %get-tuple-element.105, f32[1024]{0:T(1024)S(1)} %get-tuple-element.106, f32[1024]{0:T(1024)S(1)} %get-tuple-element.107), kind=kOutput, calls=%fused_computation.12.clone.1 | convolution fusion | flops 1222246400 | bytes 20587008 | tf_op jit(solution)/shard_map/while/body/eval_jaxpr/tqk,tkd->tqd/dot_general | solution.py:59
  540.6 0.0 copy-start.1
  540.6 1.9 divide_convert_fusion
  542.5 0.5 copy.23
  543.0 1.1 copy.27
  544.1 0.0 copy-done.1
  (20 shorter events, 0.3 us)
Async XLA Ops:
  0.0 0.8 copy-start
  66.1 9.7 %copy-start.3 = (bf16[384,1024]{1,0:T(8,128)(2,1)S(1)}, bf16[384,1024]{1,0:T(8,128)(2,1)}, u32[]{:S(2)}) copy-start(bf16[384,1024]{1,0:T(8,128)(2,1)} %param.7) | copy-start | bytes 2359300
  66.1 359.2 %all-to-all-start.1 = ((bf16[128,3,2,128,128]{4,3,2,1,0:T(8,128)(2,1)}), bf16[128,3,2,128,128]{4,3,2,1,0:T(8,128)(2,1)}, u32[]{:S(2)}, u32[]{:S(2)}) async-start(bf16[128,3,2,128,128]{4,3,2,1,0:T(8,128)(2,1)} %pad_maximum_fusion), calls=%async_computation.1 | async-start | bytes 50331648 | tf_op jit(solution)/shard_map/all_to_all | solution.py:87
  443.5 9.7 %copy-start.2 = (bf16[1,36,1,128,128]{4,3,2,1,0:T(8,128)(2,1)S(1)}, bf16[1,36,1,128,128]{4,3,2,1,0:T(8,128)(2,1)}, u32[]{:S(2)}) copy-start(bf16[1,36,1,128,128]{4,3,2,1,0:T(8,128)(2,1)} %get-tuple-element.103) | copy-start | bytes 3538948 | tf_op jit(solution)/shard_map/while
  482.0 9.7 %copy-start.2 = (bf16[1,36,1,128,128]{4,3,2,1,0:T(8,128)(2,1)S(1)}, bf16[1,36,1,128,128]{4,3,2,1,0:T(8,128)(2,1)}, u32[]{:S(2)}) copy-start(bf16[1,36,1,128,128]{4,3,2,1,0:T(8,128)(2,1)} %get-tuple-element.103) | copy-start | bytes 3538948 | tf_op jit(solution)/shard_map/while
  520.4 9.7 %copy-start.2 = (bf16[1,36,1,128,128]{4,3,2,1,0:T(8,128)(2,1)S(1)}, bf16[1,36,1,128,128]{4,3,2,1,0:T(8,128)(2,1)}, u32[]{:S(2)}) copy-start(bf16[1,36,1,128,128]{4,3,2,1,0:T(8,128)(2,1)} %get-tuple-element.103) | copy-start | bytes 3538948 | tf_op jit(solution)/shard_map/while
  540.6 3.5 copy-start.1
where the time goes:
time: 545 us; the launch traced here: 544 us
  waiting for transfers between devices  349 us (64%)
  local copies, waits for them, and re-layouts  61.8 us (11%)
  matrix products  55 us (10%)
  other arithmetic  52.5 us (10%)
  blocking collectives  15.8 us (3%)
  starting transfers between devices  9.56 us (2%)
    all_to_all x1, waiting for transfers between devices, on_device(): lax.all_to_all(lookup(requested, keys_cache, values_cache), ('grp', 'ctx'...  349 us
    dot_general x3, matrix products, attend_block(): jnp.einsum('tqk,tkd->tqd', weights.astype(jnp.bfloat16), values_now, pref...  31.4 us
    reduce_sum x3, other arithmetic, attend_block(): denominator = denominator * fading + jnp.sum(weights, axis=2)  28.9 us
    gather x3, local copies, waits for them, and re-layouts, single(): fetched[picked_one][None]  27.5 us
    gather x2, local copies, waits for them, and re-layouts, lookup(): return jnp.stack((keys_cache[requested], values_cache[requested]), axis=2)  26 us
    dot_general x3, matrix products, block_scores(): jnp.einsum('tqd,tkd->tqk', query_rows, keys_now, preferred_element_type=j...  23.6 us
    another operation x1, other arithmetic, lookup(): return jnp.stack((keys_cache[requested], values_cache[requested]), axis=2)  20.7 us
    all_to_all x1, blocking collectives, on_device(): lax.all_to_all(wanted_pages.reshape(device_count, capacity), ('grp', 'ctx...  15.8 us
  transfers between devices with their start and end apart: 1, of which 1 were waited for; matrix products, arithmetic and copies ran while one was open for 0% of the time, Pallas kernels for 0%

commit v1 on v0

v1 whole, which is shorter than its diff:
```python
import functools
import math

import jax
import jax.numpy as jnp
from jax import lax
from jax.experimental import pallas as pl
from jax.experimental.pallas import tpu as pltpu
from jax.sharding import PartitionSpec as P

HD = 128
HEADS = 8
BLOCK = 128
NB = 36
TILE_DEV = 3
BLK_DEV = 128
CAP = 3
PLANES = 4
CTX = 32
PER_GRP = NB // PLANES
KEYS = PER_GRP * BLOCK
ROWS = HEADS * BLOCK
PAIR = 2 * BLOCK
PAIRS = ROWS // PAIR
ITEMS = TILE_DEV * PAIRS
WINDOW = 16
AHEAD = 15
PEERS = CTX - 1
PLANE_STEPS = (1, 3, 2, 0)
STATS = BLOCK + 8
MESH = pl.DeviceIdType.MESH
SCALE2 = HD**-0.5 * math.log2(math.e)


def request_plan(page_ids):
    flat = page_ids.reshape(-1)
    device_of, within = flat // BLK_DEV, flat % BLK_DEV
    position = jnp.arange(flat.shape[0], dtype=jnp.int32)
    earlier = position[None, :] < position[:, None]
    rank = jnp.sum(((device_of[None, :] == device_of[:, None]) & earlier).astype(jnp.int32), axis=1)
    devices = jnp.arange(PLANES * CTX, dtype=jnp.int32)
    ranks = jnp.arange(CAP, dtype=jnp.int32)
    place = (device_of * CAP + rank)[None, None, :] == (devices[:, None] * CAP + ranks)[:, :, None]
    wanted = jnp.sum(jnp.where(place, within[None, None, :], 0), axis=2)
    tile = position // NB
    plane = device_of // CTX
    same = (plane[None, :] == plane[:, None]) & (tile[None, :] == tile[:, None]) & earlier
    order = jnp.sum(same.astype(jnp.int32), axis=1)
    slot = (device_of % CTX) * CAP + rank
    key = (plane * TILE_DEV + tile) * PER_GRP + order
    all_keys = jnp.arange(PLANES * TILE_DEV * PER_GRP, dtype=jnp.int32)
    picked = jnp.sum(jnp.where(key[None, :] == all_keys[:, None], slot[None, :], 0), axis=1)
    return wanted, picked.reshape(PLANES, TILE_DEV * PER_GRP)


def kernel(
    asked, picked, q_ref, k_hbm, v_hbm, out_ref,
    pages_k, pages_v, r0, r1, r2, r3, r4, r5, r6, r7,
    stage, q_far, scores, probs, v_turned, own, part0, part1, part2, part_far,
    load_sem, send_sem, recv_sem, q_send, q_recv, part_send, part_recv,
):
    landed = (r0, r1, r2, r3, r4, r5, r6, r7)
    parts = (part0, part1, part2, own)
    g, c = lax.axis_index("grp"), lax.axis_index("ctx")
    x, y, core = c // 8, (c // 2) % 4, c % 2

    loads = [
        pltpu.make_async_copy(k_hbm, pages_k, load_sem.at[0]),
        pltpu.make_async_copy(v_hbm, pages_v, load_sem.at[1]),
    ]
    loads[0].start()
    loads[1].start()

    def peer(i):
        m = i % 16
        a = m % 4
        b = (m // 4 + a) % 4
        return (((x + a) % 4) * 4 + (y + b) % 4) * 2 + (core + i // 16) % 2

    barrier = pltpu.get_barrier_semaphore()

    def greet(i, carry):
        pl.semaphore_signal(barrier, inc=1, device_id=(g, peer(i)), device_id_type=MESH)
        return carry

    lax.fori_loop(1, CTX, greet, 0)
    for step in (1, 2, 3):
        pl.semaphore_signal(barrier, inc=1, device_id=((g + step) % 4, c), device_id_type=MESH)
    pl.semaphore_wait(barrier, PEERS + 3)

    q_copies = []
    for p in range(3):
        q_copies.append(
            pltpu.make_async_remote_copy(
                src_ref=q_ref,
                dst_ref=q_far.at[p],
                send_sem=q_send.at[p],
                recv_sem=q_recv.at[p],
                device_id=((g + 4 - PLANE_STEPS[p]) % 4, c),
                device_id_type=MESH,
            )
        )
        q_copies[-1].start()

    def copy_of(sp, i):
        w = (sp * PEERS + i - 1) % WINDOW
        return pltpu.make_async_remote_copy(
            src_ref=stage.at[w],
            dst_ref=landed[sp].at[pl.ds(c * CAP, CAP)],
            send_sem=send_sem.at[w],
            recv_sem=recv_sem.at[sp],
            device_id=(g, peer(i)),
            device_id_type=MESH,
        )

    def first_of(sp, i):
        return ((g + PLANE_STEPS[sp // 2]) % 4) * (CTX * CAP) + peer(i) * CAP

    def push(sp, i):
        pages = (pages_k, pages_v)[sp % 2]
        number = sp * PEERS + i - 1

        @pl.when(number >= WINDOW)
        def _():
            copy_of(sp, i).wait_send()

        w, first = number % WINDOW, first_of(sp, i)
        for r in range(CAP):
            stage[w, r] = pages[asked[first + r]]
        copy_of(sp, i).start()

    def keep(sp):
        pages = (pages_k, pages_v)[sp % 2]
        for r in range(CAP):
            landed[sp][c * CAP + r] = pages[asked[first_of(sp, 0) + r]]

    def push_range(sp, low, high):
        def one(i, carry):
            push(sp, i)
            return carry

        lax.fori_loop(low, high, one, 0)

    def push_some(sp, it):
        if sp + 1 >= 8:
            return

        def one(j, carry):
            n = it * 3 + j

            @pl.when(n < PEERS - AHEAD)
            def _():
                push(sp + 1, AHEAD + 1 + n)

            if sp + 2 < 8:

                @pl.when((n >= PEERS - AHEAD) & (n < PEERS))
                def _():
                    push(sp + 2, n - (PEERS - AHEAD) + 1)

            return carry

        lax.fori_loop(0, 3, one, 0)

    def arrived(sp):
        everything = landed[sp].at[pl.ds(0, PEERS * CAP)]
        pltpu.make_async_copy(everything, everything, recv_sem.at[sp]).wait()

    def score(p, it):
        t, pair = it // PAIRS, it % PAIRS
        rows = pl.ds(pl.multiple_of(t * BLOCK, BLOCK), BLOCK)
        columns = pl.ds(pl.multiple_of(pair * PAIR, PAIR), PAIR)
        both = q_far[p, rows, columns] if p < 3 else q_ref[rows, columns]
        queries = jnp.concatenate([both[:, :HD], both[:, HD:]], axis=0)
        base = ((g + PLANE_STEPS[p]) % 4) * (TILE_DEV * PER_GRP) + t * PER_GRP
        top = jnp.full((8, PAIR), -jnp.inf, jnp.float32)
        for j in range(PER_GRP):
            keys = landed[2 * p][picked[base + j]]
            s = lax.dot_general(keys, queries, (((1,), (1,)), ((), ())), preferred_element_type=jnp.float32)
            scores[j * BLOCK : (j + 1) * BLOCK, :] = s
            top = jnp.maximum(top, jnp.max(s.reshape(BLOCK // 8, 8, PAIR), axis=0))
        largest = jnp.max(top, axis=0, keepdims=True)
        total = jnp.zeros((8, PAIR), jnp.float32)
        for j in range(PER_GRP):
            w = jnp.exp2((scores[j * BLOCK : (j + 1) * BLOCK, :] - largest) * SCALE2)
            total = total + jnp.sum(w.reshape(BLOCK // 8, 8, PAIR), axis=0)
            probs[t, j * BLOCK : (j + 1) * BLOCK, columns] = w.astype(jnp.bfloat16)
        denominator = jnp.sum(total, axis=0, keepdims=True)
        upper = lax.broadcasted_iota(jnp.int32, (8, PAIR), 0) < 4
        parts[p][t, BLOCK:STATS, columns] = jnp.where(upper, largest, denominator)

    def turn(p, t):
        base = ((g + PLANE_STEPS[p]) % 4) * (TILE_DEV * PER_GRP) + t * PER_GRP
        for j in range(PER_GRP):
            values = landed[2 * p + 1][picked[base + j]].astype(jnp.float32)
            v_turned[:, j * BLOCK : (j + 1) * BLOCK] = values.T.astype(jnp.bfloat16)

    def weigh(p, it):
        t, pair = it // PAIRS, it % PAIRS
        columns = pl.ds(pl.multiple_of(pair * PAIR, PAIR), PAIR)

        @pl.when(pair == 0)
        def _():
            turn(p, t)

        parts[p][t, 0:BLOCK, columns] = jnp.dot(
            v_turned[...], probs[t, :, columns], preferred_element_type=jnp.float32
        )

    part_copies = []
    for p in range(3):
        part_copies.append(
            pltpu.make_async_remote_copy(
                src_ref=parts[p],
                dst_ref=part_far.at[p],
                send_sem=part_send.at[p],
                recv_sem=part_recv.at[p],
                device_id=((g + PLANE_STEPS[p]) % 4, c),
                device_id_type=MESH,
            )
        )

    loads[0].wait()
    keep(0)
    push_range(0, 1, CTX)
    loads[1].wait()
    keep(1)
    push_range(1, 1, AHEAD + 1)
    for p in range(4):
        for half in range(2):
            sp = 2 * p + half
            if sp + 2 < 8:
                keep(sp + 2)
            arrived(sp)
            if half == 0 and p < 3:
                q_copies[p].wait_recv()

            def work(it, carry, sp=sp, p=p, half=half):
                push_some(sp, it)
                (score if half == 0 else weigh)(p, it)
                return carry

            lax.fori_loop(0, ITEMS, work, 0)
        if p < 3:
            part_copies[p].start()

    for p in range(3):
        q_copies[p].wait_send()
        part_copies[p].wait_send()
        part_copies[p].wait_recv()

    def drain(w, carry):
        copy_of(0, w + 1).wait_send()
        return carry

    lax.fori_loop(0, WINDOW, drain, 0)

    def finish(it, carry):
        t, pair = it // PAIRS, it % PAIRS
        columns = pl.ds(pl.multiple_of(pair * PAIR, PAIR), PAIR)
        tops = [own[t, BLOCK : BLOCK + 1, columns]] + [part_far[p, t, BLOCK : BLOCK + 1, columns] for p in range(3)]
        sums = [own[t, BLOCK + 4 : BLOCK + 5, columns]] + [
            part_far[p, t, BLOCK + 4 : BLOCK + 5, columns] for p in range(3)
        ]
        largest = functools.reduce(jnp.maximum, tops)
        fades = [jnp.exp2((top - largest) * SCALE2) for top in tops]
        denominator = sum(f * s for f, s in zip(fades, sums, strict=True))
        summed = own[t, 0:BLOCK, columns] * fades[0]
        for p in range(3):
            summed = summed + part_far[p, t, 0:BLOCK, columns] * fades[p + 1]
        summed = summed / denominator
        rows = pl.ds(pl.multiple_of(t * BLOCK, BLOCK), BLOCK)
        out_ref[rows, columns] = jnp.concatenate([summed[:, :HD].T, summed[:, HD:].T], axis=1).astype(jnp.bfloat16)
        return carry

    lax.fori_loop(0, ITEMS, finish, 0)


def on_device(queries, keys_cache, values_cache, block_list, page_table):
    wanted, picked = request_plan(page_table[block_list])
    message = jnp.concatenate(
        [wanted, jnp.repeat(picked, CTX, axis=0)], axis=1
    )
    heard = lax.all_to_all(message[:, None, :], ("grp", "ctx"), split_axis=0, concat_axis=0, tiled=True)[:, 0]
    asked = heard[:, :CAP].reshape(-1)
    places = lax.dynamic_index_in_dim(
        heard[:, CAP:].reshape(PLANES, CTX, TILE_DEV * PER_GRP), lax.axis_index("ctx"), axis=1, keepdims=False
    ).reshape(-1)
    vmem, smem = pl.BlockSpec(memory_space=pltpu.VMEM), pl.BlockSpec(memory_space=pltpu.SMEM)
    whole = pl.BlockSpec(memory_space=pl.ANY)
    half_part = pltpu.VMEM((TILE_DEV, STATS, ROWS), jnp.float32)
    return pl.pallas_call(
        kernel,
        out_shape=jax.ShapeDtypeStruct((TILE_DEV * BLOCK, ROWS), jnp.bfloat16),
        in_specs=[smem, smem, vmem, whole, whole],
        out_specs=vmem,
        scratch_shapes=[
            pltpu.VMEM((BLK_DEV, BLOCK, HD), jnp.bfloat16),
            pltpu.VMEM((BLK_DEV, BLOCK, HD), jnp.bfloat16),
            *[pltpu.VMEM((CTX * CAP, BLOCK, HD), jnp.bfloat16)] * 8,
            pltpu.VMEM((WINDOW, CAP, BLOCK, HD), jnp.bfloat16),
            pltpu.VMEM((3, TILE_DEV * BLOCK, ROWS), jnp.bfloat16),
            pltpu.VMEM((KEYS, PAIR), jnp.float32),
            pltpu.VMEM((TILE_DEV, KEYS, ROWS), jnp.bfloat16),
            pltpu.VMEM((HD, KEYS), jnp.bfloat16),
            half_part,
            half_part,
            half_part,
            half_part,
            pltpu.VMEM((3, TILE_DEV, STATS, ROWS), jnp.float32),
            pltpu.SemaphoreType.DMA((2,)),
            pltpu.SemaphoreType.DMA((WINDOW,)),
            pltpu.SemaphoreType.DMA((8,)),
            pltpu.SemaphoreType.DMA((3,)),
            pltpu.SemaphoreType.DMA((3,)),
            pltpu.SemaphoreType.DMA((3,)),
            pltpu.SemaphoreType.DMA((3,)),
        ],
        compiler_params=pltpu.CompilerParams(
            collective_id=0, has_side_effects=True, vmem_limit_bytes=66_000_000
        ),
    )(asked, places, queries, keys_cache, values_cache)


def solution(mesh):
    in_specs = (
        P(("grp", "ctx"), None),
        P(("grp", "ctx"), None, None),
        P(("grp", "ctx"), None, None),
        P(("grp", "ctx"), None),
        P(),
    )
    return jax.shard_map(
        on_device, mesh=mesh, in_specs=in_specs, out_specs=P(("grp", "ctx"), None), check_vma=False
    )
```

time: 545 us -> 348 us (0.64)
  the two profiles are of different devices: /device:TPU:50 before, /device:TPU:49 now
where the time goes in v1:
time: 348 us; the launch traced here: 347 us
  Pallas kernels  323 us (93%)
  starting transfers between devices  10.4 us (3%)
  waiting for transfers between devices  6.56 us (2%)
  local copies, waits for them, and re-layouts  5.97 us (2%)
    pallas_call x1, Pallas kernels, on_device(): pl.pallas_call(kernel, out_shape=jax.ShapeDtypeStruct((TILE_DEV * BLOCK,...  323 us
    all_to_all x1, starting transfers between devices, on_device(): lax.all_to_all(message[:, None, :], ('grp', 'ctx'), split_axis=0, concat_...  10.4 us
  transfers between devices with their start and end apart: 1, of which 1 were waited for; matrix products, arithmetic and copies ran while one was open for 0% of the time, Pallas kernels for 0%

profile of v1, /device:TPU:49, one launch (start us, length us, event | category | flops | bytes accessed | tf_op | source)
XLA Modules:
  0.0 347.4 jit_solution(14701370866096256891)
XLA Ops:
  0.0 0.0 copy-start
  0.0 0.7 compare_select_fusion
  0.7 0.1 reshape.276
  0.8 0.0 copy-done
  0.8 1.1 gather_fusion
  2.0 0.2 convert_reduce_fusion
  2.3 0.1 select_reduce_fusion.1
  2.4 0.1 reshape.269
  2.4 0.1 copy.15
  2.5 0.1 broadcast_in_dim.54
  2.7 0.1 reshape.270
  2.7 0.1 select_reduce_fusion
  2.9 0.7 copy.16
  3.6 10.4 %all-to-all-start = ((s32[128,1,30]{2,1,0:T(1,128)}), s32[128,1,30]{2,1,0:T(1,128)S(1)}, u32[]{:S(2)}, u32[]{:S(2)}) async-start(s32[128,1,30]{2,1,0:T(1,128)} %bitcast), calls=%async_computation | async-start | bytes 131072 | tf_op jit(solution)/shard_map/all_to_all | solution.py:284
  14.0 6.6 %all-to-all-done = s32[128,1,30]{2,1,0:T(1,128)S(1)} async-done(((s32[128,1,30]{2,1,0:T(1,128)}), s32[128,1,30]{2,1,0:T(1,128)S(1)}, u32[]{:S(2)}, u32[]{:S(2)}) %all-to-all-start) | async-done | bytes 15392 | tf_op jit(solution)/shard_map/all_to_all | solution.py:284
  20.6 0.1 slice.11
  20.7 0.8 reshape.271.asked
  21.5 0.7 reshape.273.picked
  22.2 323.2 %shard_map.55 = bf16[384,1024]{1,0:T(8,128)(2,1)} custom-call(s32[384]{0:T(512)} %reshape.271.asked, s32[108]{0:T(128)} %reshape.273.picked, bf16[384,1024]{1,0:T(8,128)(2,1)} %q_ref.1, bf16[128,128,128]{2,1,0:T(8,128)(2,1)} %k_hbm.1, bf16[128,128,128]{2,1,0:T(8,128)(2,1)} %v_hbm.1), custom_call_target="tpu_custom_call" | custom-call | tf_op jit(solution)/shard_map/pallas_call | solution.py:292
  345.3 2.1 copy.23
  (9 shorter events, 0.1 us)
Async XLA Ops:
  0.0 0.8 copy-start
  3.6 17.0 %all-to-all-start = ((s32[128,1,30]{2,1,0:T(1,128)}), s32[128,1,30]{2,1,0:T(1,128)S(1)}, u32[]{:S(2)}, u32[]{:S(2)}) async-start(s32[128,1,30]{2,1,0:T(1,128)} %bitcast), calls=%async_computation | async-start | bytes 131072 | tf_op jit(solution)/shard_map/all_to_all | solution.py:284

commit v2 on v1

--- a/solution.py
+++ b/solution.py
@@ -71,11 +71,17 @@
     loads[0].start()
     loads[1].start()
 
+    def walk(n):
+        return (1 + 2 * n + n // 2) % 4
+
     def peer(i):
-        m = i % 16
-        a = m % 4
-        b = (m // 4 + a) % 4
-        return (((x + a) % 4) * 4 + (y + b) % 4) * 2 + (core + i // 16) % 2
+        far = i // 16
+        m = (i + 15 + far) % 16
+        a, b = walk(m % 4), walk(m // 4)
+        b = b * (1 + 2 * (a // 3)) % 4
+        moves = (a + 3) // 4
+        b = (b + 2 * core * (moves + (1 - moves) * (b % 2))) % 4
+        return (((x + a) % 4) * 4 + (y + b) % 4) * 2 + (core + far) % 2
 
     barrier = pltpu.get_barrier_semaphore()
 

time: 348 us -> 317 us (0.911)
  the two profiles are of different devices: /device:TPU:49 before, /device:TPU:50 now
where the time goes in v2:
time: 317 us; the launch traced here: 312 us
  Pallas kernels  289 us (91%)
  starting transfers between devices  10.1 us (3%)
  local copies, waits for them, and re-layouts  5.97 us (2%)
  waiting for transfers between devices  5.8 us (2%)
    pallas_call x1, Pallas kernels, on_device(): pl.pallas_call(kernel, out_shape=jax.ShapeDtypeStruct((TILE_DEV * BLOCK,...  289 us
    all_to_all x1, starting transfers between devices, on_device(): lax.all_to_all(message[:, None, :], ('grp', 'ctx'), split_axis=0, concat_...  10.1 us
  transfers between devices with their start and end apart: 1, of which 1 were waited for; matrix products, arithmetic and copies ran while one was open for 0% of the time, Pallas kernels for 0%

profile of v2, /device:TPU:50, one launch (start us, length us, event | category | flops | bytes accessed | tf_op | source)
XLA Modules:
  0.0 312.2 jit_solution(6849841779844047056)
XLA Ops:
  0.0 0.0 copy-start
  0.0 0.7 compare_select_fusion
  0.7 0.1 reshape.276
  0.8 0.0 copy-done
  0.8 1.1 gather_fusion
  2.0 0.2 convert_reduce_fusion
  2.3 0.1 select_reduce_fusion.1
  2.4 0.1 reshape.269
  2.4 0.1 copy.15
  2.5 0.1 broadcast_in_dim.54
  2.7 0.1 reshape.270
  2.7 0.1 select_reduce_fusion
  2.9 0.7 copy.16
  3.6 10.1 %all-to-all-start = ((s32[128,1,30]{2,1,0:T(1,128)}), s32[128,1,30]{2,1,0:T(1,128)S(1)}, u32[]{:S(2)}, u32[]{:S(2)}) async-start(s32[128,1,30]{2,1,0:T(1,128)} %bitcast), calls=%async_computation | async-start | bytes 131072 | tf_op jit(solution)/shard_map/all_to_all | solution.py:290
  13.7 5.8 %all-to-all-done = s32[128,1,30]{2,1,0:T(1,128)S(1)} async-done(((s32[128,1,30]{2,1,0:T(1,128)}), s32[128,1,30]{2,1,0:T(1,128)S(1)}, u32[]{:S(2)}, u32[]{:S(2)}) %all-to-all-start) | async-done | bytes 15392 | tf_op jit(solution)/shard_map/all_to_all | solution.py:290
  19.5 0.1 slice.11
  19.6 0.8 reshape.271.asked
  20.4 0.7 reshape.273.picked
  21.1 289.0 %shard_map.55 = bf16[384,1024]{1,0:T(8,128)(2,1)} custom-call(s32[384]{0:T(512)} %reshape.271.asked, s32[108]{0:T(128)} %reshape.273.picked, bf16[384,1024]{1,0:T(8,128)(2,1)} %q_ref.1, bf16[128,128,128]{2,1,0:T(8,128)(2,1)} %k_hbm.1, bf16[128,128,128]{2,1,0:T(8,128)(2,1)} %v_hbm.1), custom_call_target="tpu_custom_call" | custom-call | tf_op jit(solution)/shard_map/pallas_call | solution.py:298
  310.1 2.1 copy.23
  (9 shorter events, 0.1 us)
Async XLA Ops:
  0.0 0.8 copy-start
  3.6 15.9 %all-to-all-start = ((s32[128,1,30]{2,1,0:T(1,128)}), s32[128,1,30]{2,1,0:T(1,128)S(1)}, u32[]{:S(2)}, u32[]{:S(2)}) async-start(s32[128,1,30]{2,1,0:T(1,128)} %bitcast), calls=%async_computation | async-start | bytes 131072 | tf_op jit(solution)/shard_map/all_to_all | solution.py:290

commit v3 on v2

--- a/solution.py
+++ b/solution.py
@@ -54,10 +54,11 @@
 
 
 def kernel(
-    asked, picked, q_ref, k_hbm, v_hbm, out_ref,
+    ask, q_ref, k_hbm, v_hbm, out_ref,
     pages_k, pages_v, r0, r1, r2, r3, r4, r5, r6, r7,
     stage, q_far, scores, probs, v_turned, own, part0, part1, part2, part_far,
-    load_sem, send_sem, recv_sem, q_send, q_recv, part_send, part_recv,
+    heard, told, asked, picked,
+    load_sem, send_sem, recv_sem, q_send, q_recv, part_send, part_recv, ask_send, ask_recv, tell_sem, note_sem,
 ):
     landed = (r0, r1, r2, r3, r4, r5, r6, r7)
     parts = (part0, part1, part2, own)
@@ -93,6 +94,51 @@
     for step in (1, 2, 3):
         pl.semaphore_signal(barrier, inc=1, device_id=((g + step) % 4, c), device_id_type=MESH)
     pl.semaphore_wait(barrier, PEERS + 3)
+
+    asks = []
+    for step in (1, 2, 3):
+        asks.append(
+            pltpu.make_async_remote_copy(
+                src_ref=ask.at[(g + step) % 4],
+                dst_ref=heard.at[g],
+                send_sem=ask_send.at[step],
+                recv_sem=ask_recv.at[step],
+                device_id=((g + step) % 4, c),
+                device_id_type=MESH,
+            )
+        )
+        asks[-1].start()
+    asks.append(pltpu.make_async_copy(ask.at[g], heard.at[g], ask_send.at[0]))
+    asks[-1].start()
+    for copy in asks:
+        copy.wait()
+
+    def tell(i, carry):
+        pltpu.make_async_remote_copy(
+            src_ref=heard.at[:, peer(i)],
+            dst_ref=told.at[c],
+            send_sem=tell_sem.at[0],
+            recv_sem=tell_sem.at[1],
+            device_id=(g, peer(i)),
+            device_id_type=MESH,
+        ).start()
+        return carry
+
+    lax.fori_loop(1, CTX, tell, 0)
+    note = [
+        pltpu.make_async_copy(heard.at[:, c], told.at[c], note_sem.at[0]),
+        pltpu.make_async_copy(heard.at[:, CTX], picked, note_sem.at[1]),
+    ]
+    for copy in note:
+        copy.start()
+    for copy in note:
+        copy.wait()
+    for way in range(2):
+        everyone = told.at[pl.ds(0, PEERS)]
+        pltpu.make_async_copy(everyone, everyone, tell_sem.at[way]).wait()
+    note = pltpu.make_async_copy(told, asked, note_sem.at[0])
+    note.start()
+    note.wait()
 
     q_copies = []
     for p in range(3):
@@ -119,8 +165,8 @@
             device_id_type=MESH,
         )
 
-    def first_of(sp, i):
-        return ((g + PLANE_STEPS[sp // 2]) % 4) * (CTX * CAP) + peer(i) * CAP
+    def plane_of(p):
+        return (g + PLANE_STEPS[p]) % 4
 
     def push(sp, i):
         pages = (pages_k, pages_v)[sp % 2]
@@ -130,15 +176,15 @@
         def _():
             copy_of(sp, i).wait_send()
 
-        w, first = number % WINDOW, first_of(sp, i)
+        w, who = number % WINDOW, peer(i)
         for r in range(CAP):
-            stage[w, r] = pages[asked[first + r]]
+            stage[w, r] = pages[asked[who, plane_of(sp // 2), 0, r]]
         copy_of(sp, i).start()
 
     def keep(sp):
         pages = (pages_k, pages_v)[sp % 2]
         for r in range(CAP):
-            landed[sp][c * CAP + r] = pages[asked[first_of(sp, 0) + r]]
+            landed[sp][c * CAP + r] = pages[asked[c, plane_of(sp // 2), 0, r]]
 
     def push_range(sp, low, high):
         def one(i, carry):
@@ -178,10 +224,9 @@
         columns = pl.ds(pl.multiple_of(pair * PAIR, PAIR), PAIR)
         both = q_far[p, rows, columns] if p < 3 else q_ref[rows, columns]
         queries = jnp.concatenate([both[:, :HD], both[:, HD:]], axis=0)
-        base = ((g + PLANE_STEPS[p]) % 4) * (TILE_DEV * PER_GRP) + t * PER_GRP
         top = jnp.full((8, PAIR), -jnp.inf, jnp.float32)
         for j in range(PER_GRP):
-            keys = landed[2 * p][picked[base + j]]
+            keys = landed[2 * p][picked[plane_of(p), 0, t * PER_GRP + j]]
             s = lax.dot_general(keys, queries, (((1,), (1,)), ((), ())), preferred_element_type=jnp.float32)
             scores[j * BLOCK : (j + 1) * BLOCK, :] = s
             top = jnp.maximum(top, jnp.max(s.reshape(BLOCK // 8, 8, PAIR), axis=0))
@@ -195,11 +240,19 @@
         upper = lax.broadcasted_iota(jnp.int32, (8, PAIR), 0) < 4
         parts[p][t, BLOCK:STATS, columns] = jnp.where(upper, largest, denominator)
 
-    def turn(p, t):
-        base = ((g + PLANE_STEPS[p]) % 4) * (TILE_DEV * PER_GRP) + t * PER_GRP
+    def gather_values(p, t):
         for j in range(PER_GRP):
-            values = landed[2 * p + 1][picked[base + j]].astype(jnp.float32)
-            v_turned[:, j * BLOCK : (j + 1) * BLOCK] = values.T.astype(jnp.bfloat16)
+            v_turned[:, j * BLOCK : (j + 1) * BLOCK] = landed[2 * p + 1][picked[plane_of(p), 0, t * PER_GRP + j]]
+
+    def part_copy(p, t):
+        return pltpu.make_async_remote_copy(
+            src_ref=parts[p].at[t],
+            dst_ref=part_far.at[p, t],
+            send_sem=part_send.at[p, t],
+            recv_sem=part_recv.at[p, t],
+            device_id=(plane_of(p), c),
+            device_id_type=MESH,
+        )
 
     def weigh(p, it):
         t, pair = it // PAIRS, it % PAIRS
@@ -207,29 +260,53 @@
 
         @pl.when(pair == 0)
         def _():
-            turn(p, t)
-
-        parts[p][t, 0:BLOCK, columns] = jnp.dot(
-            v_turned[...], probs[t, :, columns], preferred_element_type=jnp.float32
-        )
-
-    part_copies = []
-    for p in range(3):
-        part_copies.append(
-            pltpu.make_async_remote_copy(
-                src_ref=parts[p],
-                dst_ref=part_far.at[p],
-                send_sem=part_send.at[p],
-                recv_sem=part_recv.at[p],
-                device_id=((g + PLANE_STEPS[p]) % 4, c),
-                device_id_type=MESH,
-            )
-        )
+            gather_values(p, t)
+
+        summed = jnp.dot(v_turned[...], probs[t, :, columns], preferred_element_type=jnp.float32)
+        if p < 3:
+            parts[p][t, 0:BLOCK, columns] = summed
+
+            @pl.when(pair == PAIRS - 1)
+            def _():
+                part_copy(p, t).start()
+        else:
+            result = summed * part_far[0, t, BLOCK : BLOCK + 1, columns] + part_far[0, t, 0:BLOCK, columns]
+            rows = pl.ds(pl.multiple_of(t * BLOCK, BLOCK), BLOCK)
+            out_ref[rows, columns] = jnp.concatenate([result[:, :HD].T, result[:, HD:].T], axis=1).astype(jnp.bfloat16)
+
+    def settle(it, carry):
+        t, pair = it // PAIRS, it % PAIRS
+        columns = pl.ds(pl.multiple_of(pair * PAIR, PAIR), PAIR)
+        stats = [own[t, BLOCK:STATS, columns]] + [part_far[p, t, BLOCK:STATS, columns] for p in range(3)]
+        tops, sums = [v[0:1] for v in stats], [v[4:5] for v in stats]
+        largest = functools.reduce(jnp.maximum, tops)
+        fades = [jnp.exp2((top - largest) * SCALE2) for top in tops]
+        denominator = sum(f * v for f, v in zip(fades, sums, strict=True))
+        fades = [f / denominator for f in fades]
+        rest = part_far[0, t, 0:BLOCK, columns] * fades[1]
+        for p in (1, 2):
+            rest = rest + part_far[p, t, 0:BLOCK, columns] * fades[p + 1]
+        part_far[0, t, 0:BLOCK, columns] = rest
+        part_far[0, t, BLOCK:STATS, columns] = jnp.broadcast_to(fades[0], (8, PAIR))
+        return carry
 
     loads[0].wait()
     keep(0)
-    push_range(0, 1, CTX)
+    push_range(0, 1, WINDOW + 1)
     loads[1].wait()
+
+    def turn(i):
+        pages_v[i] = pages_v[i].astype(jnp.float32).T.astype(jnp.bfloat16)
+
+    def push_and_turn(i, carry):
+        push(0, i)
+        for n in range(8):
+            turn((i - WINDOW - 1) * 8 + n)
+        return carry
+
+    lax.fori_loop(WINDOW + 1, CTX, push_and_turn, 0)
+    for n in range((PEERS - WINDOW) * 8, BLK_DEV):
+        turn(n)
     keep(1)
     push_range(1, 1, AHEAD + 1)
     for p in range(4):
@@ -237,6 +314,11 @@
             sp = 2 * p + half
             if sp + 2 < 8:
                 keep(sp + 2)
+            if sp == 7:
+                for far in range(3):
+                    for t in range(TILE_DEV):
+                        part_copy(far, t).wait_recv()
+                lax.fori_loop(0, ITEMS, settle, 0)
             arrived(sp)
             if half == 0 and p < 3:
                 q_copies[p].wait_recv()
@@ -247,13 +329,11 @@
                 return carry
 
             lax.fori_loop(0, ITEMS, work, 0)
-        if p < 3:
-            part_copies[p].start()
 
     for p in range(3):
         q_copies[p].wait_send()
-        part_copies[p].wait_send()
-        part_copies[p].wait_recv()
+        for t in range(TILE_DEV):
+            part_copy(p, t).wait_send()
 
     def drain(w, carry):
         copy_of(0, w + 1).wait_send()
@@ -261,44 +341,24 @@
 
     lax.fori_loop(0, WINDOW, drain, 0)
 
-    def finish(it, carry):
-        t, pair = it // PAIRS, it % PAIRS
-        columns = pl.ds(pl.multiple_of(pair * PAIR, PAIR), PAIR)
-        tops = [own[t, BLOCK : BLOCK + 1, columns]] + [part_far[p, t, BLOCK : BLOCK + 1, columns] for p in range(3)]
-        sums = [own[t, BLOCK + 4 : BLOCK + 5, columns]] + [
-            part_far[p, t, BLOCK + 4 : BLOCK + 5, columns] for p in range(3)
-        ]
-        largest = functools.reduce(jnp.maximum, tops)
-        fades = [jnp.exp2((top - largest) * SCALE2) for top in tops]
-        denominator = sum(f * s for f, s in zip(fades, sums, strict=True))
-        summed = own[t, 0:BLOCK, columns] * fades[0]
-        for p in range(3):
-            summed = summed + part_far[p, t, 0:BLOCK, columns] * fades[p + 1]
-        summed = summed / denominator
-        rows = pl.ds(pl.multiple_of(t * BLOCK, BLOCK), BLOCK)
-        out_ref[rows, columns] = jnp.concatenate([summed[:, :HD].T, summed[:, HD:].T], axis=1).astype(jnp.bfloat16)
-        return carry
-
-    lax.fori_loop(0, ITEMS, finish, 0)
-
 
 def on_device(queries, keys_cache, values_cache, block_list, page_table):
     wanted, picked = request_plan(page_table[block_list])
-    message = jnp.concatenate(
-        [wanted, jnp.repeat(picked, CTX, axis=0)], axis=1
-    )
-    heard = lax.all_to_all(message[:, None, :], ("grp", "ctx"), split_axis=0, concat_axis=0, tiled=True)[:, 0]
-    asked = heard[:, :CAP].reshape(-1)
-    places = lax.dynamic_index_in_dim(
-        heard[:, CAP:].reshape(PLANES, CTX, TILE_DEV * PER_GRP), lax.axis_index("ctx"), axis=1, keepdims=False
-    ).reshape(-1)
-    vmem, smem = pl.BlockSpec(memory_space=pltpu.VMEM), pl.BlockSpec(memory_space=pltpu.SMEM)
+    lanes = BLOCK
+    ask = jnp.concatenate(
+        [
+            jnp.pad(wanted, ((0, 0), (0, lanes - CAP))).reshape(PLANES, CTX, lanes),
+            jnp.pad(picked, ((0, 0), (0, lanes - TILE_DEV * PER_GRP)))[:, None],
+        ],
+        axis=1,
+    )[:, :, None]
+    vmem = pl.BlockSpec(memory_space=pltpu.VMEM)
     whole = pl.BlockSpec(memory_space=pl.ANY)
     half_part = pltpu.VMEM((TILE_DEV, STATS, ROWS), jnp.float32)
     return pl.pallas_call(
         kernel,
         out_shape=jax.ShapeDtypeStruct((TILE_DEV * BLOCK, ROWS), jnp.bfloat16),
-        in_specs=[smem, smem, vmem, whole, whole],
+        in_specs=[vmem, vmem, whole, whole],
         out_specs=vmem,
         scratch_shapes=[
             pltpu.VMEM((BLK_DEV, BLOCK, HD), jnp.bfloat16),
@@ -314,18 +374,26 @@
             half_part,
             half_part,
             pltpu.VMEM((3, TILE_DEV, STATS, ROWS), jnp.float32),
+            pltpu.VMEM((PLANES, CTX + 1, 1, BLOCK), jnp.int32),
+            pltpu.VMEM((CTX, PLANES, 1, BLOCK), jnp.int32),
+            pltpu.SMEM((CTX, PLANES, 1, BLOCK), jnp.int32),
+            pltpu.SMEM((PLANES, 1, BLOCK), jnp.int32),
             pltpu.SemaphoreType.DMA((2,)),
             pltpu.SemaphoreType.DMA((WINDOW,)),
             pltpu.SemaphoreType.DMA((8,)),
             pltpu.SemaphoreType.DMA((3,)),
             pltpu.SemaphoreType.DMA((3,)),
-            pltpu.SemaphoreType.DMA((3,)),
-            pltpu.SemaphoreType.DMA((3,)),
+            pltpu.SemaphoreType.DMA((3, TILE_DEV)),
+            pltpu.SemaphoreType.DMA((3, TILE_DEV)),
+            pltpu.SemaphoreType.DMA((4,)),
+            pltpu.SemaphoreType.DMA((4,)),
+            pltpu.SemaphoreType.DMA((2,)),
+            pltpu.SemaphoreType.DMA((2,)),
         ],
         compiler_params=pltpu.CompilerParams(
             collective_id=0, has_side_effects=True, vmem_limit_bytes=66_000_000
         ),
-    )(asked, places, queries, keys_cache, values_cache)
+    )(ask, queries, keys_cache, values_cache)
 
 
 def solution(mesh):

time: 317 us -> 308 us (0.972)
  starting transfers between devices: 10.1 us -> 0 us
  Pallas kernels: 289 us -> 298 us
  waiting for transfers between devices: 5.8 us -> 0 us
    all_to_all x1 -> x0, starting transfers between devices: 10.1 us -> none  [on_device(): lax.all_to_all(message[:, None, :], ('grp', 'ctx'), split_axis=0, concat_...]
    pallas_call x1, Pallas kernels: 289 us -> 298 us  [on_device(): pl.pallas_call(kernel, out_shape=jax.ShapeDtypeStruct((TILE_DEV * BLOCK,...]
    all_to_all x1 -> x0, waiting for transfers between devices: 5.8 us -> none  [on_device(): lax.all_to_all(message[:, None, :], ('grp', 'ctx'), split_axis=0, concat_...]
  transfers between devices with their start and end apart: 1 -> 0, of which waited for: 1 -> 0; matrix products, arithmetic and copies ran while one was open for 0% -> 0% of each run, Pallas kernels for 0% -> 0%
where the time goes in v3:
time: 308 us; the launch traced here: 303 us
  Pallas kernels  298 us (97%)
  local copies, waits for them, and re-layouts  4.21 us (1%)
    pallas_call x1, Pallas kernels, on_device(): pl.pallas_call(kernel, out_shape=jax.ShapeDtypeStruct((TILE_DEV * BLOCK,...  298 us

profile of v3, /device:TPU:50, one launch (start us, length us, event | category | flops | bytes accessed | tf_op | source)
XLA Modules:
  0.0 303.3 jit_solution(10630687217841086558)
XLA Ops:
  0.0 0.0 copy-start
  0.0 0.7 compare_select_fusion
  0.7 0.1 reshape.263
  0.8 0.0 copy-done
  0.8 1.1 gather_fusion
  2.0 0.2 convert_reduce_fusion
  2.3 0.1 select_reduce_fusion
  2.4 0.1 select_reduce_fusion.1
  2.5 0.1 reshape.260
  2.6 0.1 copy.14
  2.7 0.7 copy.11.ask
  3.4 297.8 %shard_map.55 = bf16[384,1024]{1,0:T(8,128)(2,1)} custom-call(s32[4,33,1,128]{3,2,1,0:T(1,128)} %copy.11.ask, bf16[384,1024]{1,0:T(8,128)(2,1)} %q_ref.1, bf16[128,128,128]{2,1,0:T(8,128)(2,1)} %k_hbm.1, bf16[128,128,128]{2,1,0:T(8,128)(2,1)} %v_hbm.1), custom_call_target="tpu_custom_call" | custom-call | tf_op jit(solution)/shard_map/pallas_call | solution.py:358
  301.3 2.1 copy.16
  (10 shorter events, 0.1 us)
Async XLA Ops:
  0.0 0.8 copy-start

commit v4 on v3

--- a/solution.py
+++ b/solution.py
@@ -25,6 +25,10 @@
 ITEMS = TILE_DEV * PAIRS
 WINDOW = 16
 AHEAD = 15
+EARLY = 12
+OWN_KEYS = 6
+FIRST = WINDOW - EARLY + 1
+TURNS = BLK_DEV // (32 - FIRST)
 PEERS = CTX - 1
 PLANE_STEPS = (1, 3, 2, 0)
 STATS = BLOCK + 8
@@ -54,11 +58,12 @@
 
 
 def kernel(
-    ask, q_ref, k_hbm, v_hbm, out_ref,
+    ask, q_hbm, k_hbm, v_hbm, out_ref,
+    q_ref, near, near_asked,
     pages_k, pages_v, r0, r1, r2, r3, r4, r5, r6, r7,
     stage, q_far, scores, probs, v_turned, own, part0, part1, part2, part_far,
     heard, told, asked, picked,
-    load_sem, send_sem, recv_sem, q_send, q_recv, part_send, part_recv, ask_send, ask_recv, tell_sem, note_sem,
+    load_sem, send_sem, recv_sem, q_send, q_recv, part_send, part_recv, ask_send, ask_recv, tell_sem, near_sem, note_sem,
 ):
     landed = (r0, r1, r2, r3, r4, r5, r6, r7)
     parts = (part0, part1, part2, own)
@@ -68,8 +73,10 @@
     loads = [
         pltpu.make_async_copy(k_hbm, pages_k, load_sem.at[0]),
         pltpu.make_async_copy(v_hbm, pages_v, load_sem.at[1]),
+        pltpu.make_async_copy(q_hbm, q_ref, load_sem.at[2]),
     ]
     loads[0].start()
+    loads[2].start()
     loads[1].start()
 
     def walk(n):
@@ -94,6 +101,43 @@
     for step in (1, 2, 3):
         pl.semaphore_signal(barrier, inc=1, device_id=((g + step) % 4, c), device_id_type=MESH)
     pl.semaphore_wait(barrier, PEERS + 3)
+
+    def plane_of(p):
+        return (g + PLANE_STEPS[p]) % 4
+
+    def number_of(sp, i):
+        return sp * PEERS + i - 1 + (EARLY if sp < OWN_KEYS else 0)
+
+    def copy_of(sp, i, number):
+        w = number % WINDOW
+        return pltpu.make_async_remote_copy(
+            src_ref=stage.at[w],
+            dst_ref=landed[sp].at[pl.ds(c * CAP, CAP)],
+            send_sem=send_sem.at[w],
+            recv_sem=recv_sem.at[sp],
+            device_id=(g, peer(i)),
+            device_id_type=MESH,
+        )
+
+    def push(sp, i):
+        pages = (pages_k, pages_v)[sp % 2]
+        number = number_of(sp, i)
+
+        @pl.when(number >= WINDOW)
+        def _():
+            copy_of(sp, i, number).wait_send()
+
+        w, who = number % WINDOW, peer(i)
+        for r in range(CAP):
+            stage[w, r] = pages[asked[who, plane_of(sp // 2), 0, r]]
+        copy_of(sp, i, number).start()
+
+    def push_early(i, carry):
+        who = peer(i)
+        for r in range(CAP):
+            stage[i - 1, r] = pages_k[near_asked[who, 0, r]]
+        copy_of(OWN_KEYS, i, i - 1).start()
+        return carry
 
     asks = []
     for step in (1, 2, 3):
@@ -110,6 +154,21 @@
         asks[-1].start()
     asks.append(pltpu.make_async_copy(ask.at[g], heard.at[g], ask_send.at[0]))
     asks[-1].start()
+
+    def tell_near(i, carry):
+        pltpu.make_async_remote_copy(
+            src_ref=ask.at[g, peer(i)],
+            dst_ref=near.at[c],
+            send_sem=near_sem.at[0],
+            recv_sem=near_sem.at[1],
+            device_id=(g, peer(i)),
+            device_id_type=MESH,
+        ).start()
+        return carry
+
+    own_near = pltpu.make_async_copy(ask.at[g, c], near.at[c], near_sem.at[2])
+    own_near.start()
+    lax.fori_loop(1, CTX, tell_near, 0)
     for copy in asks:
         copy.wait()
 
@@ -125,20 +184,21 @@
         return carry
 
     lax.fori_loop(1, CTX, tell, 0)
-    note = [
-        pltpu.make_async_copy(heard.at[:, c], told.at[c], note_sem.at[0]),
-        pltpu.make_async_copy(heard.at[:, CTX], picked, note_sem.at[1]),
-    ]
-    for copy in note:
-        copy.start()
-    for copy in note:
-        copy.wait()
+    own_list = pltpu.make_async_copy(heard.at[:, c], told.at[c], note_sem.at[0])
+    own_picks = pltpu.make_async_copy(heard.at[:, CTX], picked, note_sem.at[1])
+    own_list.start()
+    own_picks.start()
     for way in range(2):
-        everyone = told.at[pl.ds(0, PEERS)]
-        pltpu.make_async_copy(everyone, everyone, tell_sem.at[way]).wait()
-    note = pltpu.make_async_copy(told, asked, note_sem.at[0])
-    note.start()
-    note.wait()
+        everyone = near.at[pl.ds(0, PEERS)]
+        pltpu.make_async_copy(everyone, everyone, near_sem.at[way]).wait()
+    own_near.wait()
+    near_note = pltpu.make_async_copy(near, near_asked, near_sem.at[2])
+    near_note.start()
+    near_note.wait()
+    loads[0].wait()
+    lax.fori_loop(1, EARLY + 1, push_early, 0)
+
+    loads[2].wait()
 
     q_copies = []
     for p in range(3):
@@ -154,32 +214,14 @@
         )
         q_copies[-1].start()
 
-    def copy_of(sp, i):
-        w = (sp * PEERS + i - 1) % WINDOW
-        return pltpu.make_async_remote_copy(
-            src_ref=stage.at[w],
-            dst_ref=landed[sp].at[pl.ds(c * CAP, CAP)],
-            send_sem=send_sem.at[w],
-            recv_sem=recv_sem.at[sp],
-            device_id=(g, peer(i)),
-            device_id_type=MESH,
-        )
-
-    def plane_of(p):
-        return (g + PLANE_STEPS[p]) % 4
-
-    def push(sp, i):
-        pages = (pages_k, pages_v)[sp % 2]
-        number = sp * PEERS + i - 1
-
-        @pl.when(number >= WINDOW)
-        def _():
-            copy_of(sp, i).wait_send()
-
-        w, who = number % WINDOW, peer(i)
-        for r in range(CAP):
-            stage[w, r] = pages[asked[who, plane_of(sp // 2), 0, r]]
-        copy_of(sp, i).start()
+    own_list.wait()
+    own_picks.wait()
+    for way in range(2):
+        everyone = told.at[pl.ds(0, PEERS)]
+        pltpu.make_async_copy(everyone, everyone, tell_sem.at[way]).wait()
+    note = pltpu.make_async_copy(told, asked, note_sem.at[0])
+    note.start()
+    note.wait()
 
     def keep(sp):
         pages = (pages_k, pages_v)[sp % 2]
@@ -206,7 +248,9 @@
 
             if sp + 2 < 8:
 
-                @pl.when((n >= PEERS - AHEAD) & (n < PEERS))
+                begun = EARLY if sp + 2 == OWN_KEYS else 0
+
+                @pl.when((n >= PEERS - AHEAD + begun) & (n < PEERS))
                 def _():
                     push(sp + 2, n - (PEERS - AHEAD) + 1)
 
@@ -290,9 +334,8 @@
         part_far[0, t, BLOCK:STATS, columns] = jnp.broadcast_to(fades[0], (8, PAIR))
         return carry
 
-    loads[0].wait()
     keep(0)
-    push_range(0, 1, WINDOW + 1)
+    push_range(0, 1, WINDOW - EARLY + 1)
     loads[1].wait()
 
     def turn(i):
@@ -300,12 +343,12 @@
 
     def push_and_turn(i, carry):
         push(0, i)
-        for n in range(8):
-            turn((i - WINDOW - 1) * 8 + n)
-        return carry
-
-    lax.fori_loop(WINDOW + 1, CTX, push_and_turn, 0)
-    for n in range((PEERS - WINDOW) * 8, BLK_DEV):
+        for n in range(TURNS):
+            turn((i - FIRST) * TURNS + n)
+        return carry
+
+    lax.fori_loop(FIRST, CTX, push_and_turn, 0)
+    for n in range((CTX - FIRST) * TURNS, BLK_DEV):
         turn(n)
     keep(1)
     push_range(1, 1, AHEAD + 1)
@@ -336,7 +379,7 @@
             part_copy(p, t).wait_send()
 
     def drain(w, carry):
-        copy_of(0, w + 1).wait_send()
+        copy_of(0, 1, w).wait_send()
         return carry
 
     lax.fori_loop(0, WINDOW, drain, 0)
@@ -358,9 +401,12 @@
     return pl.pallas_call(
         kernel,
         out_shape=jax.ShapeDtypeStruct((TILE_DEV * BLOCK, ROWS), jnp.bfloat16),
-        in_specs=[vmem, vmem, whole, whole],
+        in_specs=[vmem, whole, whole, whole],
         out_specs=vmem,
         scratch_shapes=[
+            pltpu.VMEM((TILE_DEV * BLOCK, ROWS), jnp.bfloat16),
+            pltpu.VMEM((CTX, 1, BLOCK), jnp.int32),
+            pltpu.SMEM((CTX, 1, BLOCK), jnp.int32),
             pltpu.VMEM((BLK_DEV, BLOCK, HD), jnp.bfloat16),
             pltpu.VMEM((BLK_DEV, BLOCK, HD), jnp.bfloat16),
             *[pltpu.VMEM((CTX * CAP, BLOCK, HD), jnp.bfloat16)] * 8,
@@ -378,7 +424,7 @@
             pltpu.VMEM((CTX, PLANES, 1, BLOCK), jnp.int32),
             pltpu.SMEM((CTX, PLANES, 1, BLOCK), jnp.int32),
             pltpu.SMEM((PLANES, 1, BLOCK), jnp.int32),
-            pltpu.SemaphoreType.DMA((2,)),
+            pltpu.SemaphoreType.DMA((3,)),
             pltpu.SemaphoreType.DMA((WINDOW,)),
             pltpu.SemaphoreType.DMA((8,)),
             pltpu.SemaphoreType.DMA((3,)),
@@ -388,6 +434,7 @@
             pltpu.SemaphoreType.DMA((4,)),
             pltpu.SemaphoreType.DMA((4,)),
             pltpu.SemaphoreType.DMA((2,)),
+            pltpu.SemaphoreType.DMA((3,)),
             pltpu.SemaphoreType.DMA((2,)),
         ],
         compiler_params=pltpu.CompilerParams(

time: 308 us -> 307 us (level)
  no operation moved by 1% of the time
where the time goes in v4:
time: 307 us; the launch traced here: 302 us
  Pallas kernels  296 us (96%)
  local copies, waits for them, and re-layouts  4.21 us (1%)
    pallas_call x1, Pallas kernels, on_device(): pl.pallas_call(kernel, out_shape=jax.ShapeDtypeStruct((TILE_DEV * BLOCK,...  296 us

profile of v4, /device:TPU:50, one launch (start us, length us, event | category | flops | bytes accessed | tf_op | source)
XLA Modules:
  0.0 301.5 jit_solution(667374782736780718)
XLA Ops:
  0.0 0.0 copy-start
  0.0 0.7 compare_select_fusion
  0.7 0.1 reshape.263
  0.8 0.0 copy-done
  0.8 1.1 gather_fusion
  2.0 0.2 convert_reduce_fusion
  2.3 0.1 select_reduce_fusion
  2.4 0.1 select_reduce_fusion.1
  2.5 0.1 reshape.260
  2.6 0.1 copy.14
  2.7 0.7 copy.11.ask
  3.4 296.0 %shard_map.55 = bf16[384,1024]{1,0:T(8,128)(2,1)} custom-call(s32[4,33,1,128]{3,2,1,0:T(1,128)} %copy.11.ask, bf16[384,1024]{1,0:T(8,128)(2,1)} %q_hbm.1, bf16[128,128,128]{2,1,0:T(8,128)(2,1)} %k_hbm.1, bf16[128,128,128]{2,1,0:T(8,128)(2,1)} %v_hbm.1), custom_call_target="tpu_custom_call" | custom-call | tf_op jit(solution)/shard_map/pallas_call | solution.py:401
  299.5 2.1 copy.16
  (10 shorter events, 0.1 us)
Async XLA Ops:
  0.0 0.8 copy-start

commit v5 on v4

--- a/solution.py
+++ b/solution.py
@@ -25,7 +25,7 @@
 ITEMS = TILE_DEV * PAIRS
 WINDOW = 16
 AHEAD = 15
-EARLY = 12
+EARLY = 15
 OWN_KEYS = 6
 FIRST = WINDOW - EARLY + 1
 TURNS = BLK_DEV // (32 - FIRST)

time: 307 us -> 307 us (level)
  no operation moved by 1% of the time
where the time goes in v5:
time: 307 us; the launch traced here: 303 us
  Pallas kernels  297 us (97%)
  local copies, waits for them, and re-layouts  4.21 us (1%)
    pallas_call x1, Pallas kernels, on_device(): pl.pallas_call(kernel, out_shape=jax.ShapeDtypeStruct((TILE_DEV * BLOCK,...  297 us

profile of v5, /device:TPU:50, one launch (start us, length us, event | category | flops | bytes accessed | tf_op | source)
XLA Modules:
  0.0 302.6 jit_solution(15544306394512981528)
XLA Ops:
  0.0 0.0 copy-start
  0.0 0.7 compare_select_fusion
  0.7 0.1 reshape.263
  0.8 0.0 copy-done
  0.8 1.1 gather_fusion
  2.0 0.2 convert_reduce_fusion
  2.3 0.1 select_reduce_fusion
  2.4 0.1 select_reduce_fusion.1
  2.5 0.1 reshape.260
  2.6 0.1 copy.14
  2.7 0.7 copy.11.ask
  3.4 297.1 %shard_map.55 = bf16[384,1024]{1,0:T(8,128)(2,1)} custom-call(s32[4,33,1,128]{3,2,1,0:T(1,128)} %copy.11.ask, bf16[384,1024]{1,0:T(8,128)(2,1)} %q_hbm.1, bf16[128,128,128]{2,1,0:T(8,128)(2,1)} %k_hbm.1, bf16[128,128,128]{2,1,0:T(8,128)(2,1)} %v_hbm.1), custom_call_target="tpu_custom_call" | custom-call | tf_op jit(solution)/shard_map/pallas_call | solution.py:401
  300.6 2.1 copy.16
  (10 shorter events, 0.1 us)
Async XLA Ops:
  0.0 0.8 copy-start
